TPU v7x, 256 devices: a whole 4x4x8 slice. The times are simulated.
256 devices in a mesh: grp: 16 (over y_hi, x, core), tp: 16 (over y_lo, z).
Axes of the slice: x: 4, y: 4 (y_hi: 2, y_lo: 2; y = y_hi * 2 + y_lo), z: 8, core: 2. Of those that a mesh axis runs over, the one named last changes fastest.
Arguments:
- x_rows: bfloat16 [16384, 4096], P(('grp', 'tp')), may hold values from -6 to 6
- norm_gain: float32 [4096], replicated, may hold values from 0.1 to 1.9
- w_query: bfloat16 [4096, 4096], P(None, 'tp'), may hold values from -0.25 to 0.25
- w_keyval: bfloat16 [4096, 2, 1024], P(None, None, 'tp'), may hold values from -0.09375 to 0.09375
- w_out: bfloat16 [4096, 4096], P('tp'), may hold values from -0.75 to 0.75
- prefix_cache: bfloat16 [32, 128, 2, 1024], P('grp', None, None, 'tp'), may hold values from -70 to 70, as said below
- page_table: int32 [32], replicated, may hold values from 0 to 31, each once
- request_ids: int32 [16384], replicated, may hold values from 0 to 31, never falling along the last dimension, each value on 1 to 1024 neighbouring positions
Outputs:
- attn_out: bfloat16 [16384, 4096], P(('grp', 'tp'))
Inputs may be any that keep to these rules, and one draw needn't show every extreme that they name: `request_ids`: request ids never fall along the stream; each of the 32 requests has 1 to 1024 tokens, one exactly 1024. `page_table`: a permutation; physical page f belongs to group f // 2. `prefix_cache`: keys are stored already rotated for their positions.
All inputs are finite; a program needn't handle non-finite values.
Results may differ from a plain program's by a relative error of at most 0.025.
The roundings to bfloat16 on the way count: a program that leaves them out, or rounds other values in their place, can miss the bound.
Values may be sent and summed in bfloat16 or wider, within the bound.
A program may use at most 64 MiB of HBM per device.

v0:
```python
import jax
import jax.numpy as jnp
from jax import lax
from jax.sharding import PartitionSpec as P

KVH = 8
HD = 128
SINKS = 4


def swapped(block, axis, apart):
    count = lax.axis_size(axis)
    route = []
    for low in range(count):
        high = low | 1 << apart
        if high != low and high < count:
            route += [(low, high), (high, low)]
    return lax.ppermute(block, axis, route)


def shifted(block, axis, distance):
    devices = range(lax.axis_size(axis))
    route = [(i - distance, i) for i in devices if i - distance in devices]
    return lax.ppermute(block, axis, route)


def rotate(values, positions):
    half = HD // 2
    freqs = 500000.0 ** (-jnp.arange(half, dtype=jnp.float32) * 2.0 / HD)
    angles = positions.astype(jnp.float32)[:, None] * freqs[None, :]
    cosine = jnp.cos(angles)[:, None, :]
    sine = jnp.sin(angles)[:, None, :]
    first = values[..., :half]
    second = values[..., half:]
    return jnp.concatenate(
        [first * cosine - second * sine, second * cosine + first * sine], axis=-1
    )


def segment_first(request_ids, wanted, count):
    labels = jnp.arange(count, dtype=jnp.int32)
    counts = jnp.sum((request_ids[:, None] == labels[None, :]).astype(jnp.int32), axis=0)
    starts = jnp.cumsum(counts) - counts
    match = wanted[:, None] == labels[None, :]
    return jnp.sum(jnp.where(match, starts[None, :], 0), axis=1)


def join_pair(lower, mine, peer):
    return jnp.where(
        lower, jnp.concatenate([mine, peer], axis=2), jnp.concatenate([peer, mine], axis=2)
    )


def fold_block(state, queries, keys, values, visible):
    run_max, run_sum, run_acc = state
    scores = jnp.einsum(
        "qgrd,kgd->qgrk", queries, keys, preferred_element_type=jnp.float32
    ) * HD ** (-0.5)
    allowed = visible[:, None, None, :]
    scores = jnp.where(allowed, scores, -1e30)
    new_max = jnp.maximum(run_max, jnp.max(scores, axis=-1))
    weights = jnp.where(allowed, jnp.exp(scores - new_max[..., None]), 0.0)
    factor = jnp.exp(run_max - new_max)
    new_sum = run_sum * factor + jnp.sum(weights, axis=-1)
    new_acc = run_acc * factor[..., None] + jnp.einsum(
        "qgrk,kgd->qgrd", weights.astype(jnp.bfloat16), values, preferred_element_type=jnp.float32
    )
    return (new_max, new_sum, new_acc)


def fold_all(
    state, queries, query_pos, query_seg, query_index, keys, values, visible_fn, block_rows
):
    blocks = queries.shape[0] // block_rows

    def in_blocks(array):
        return array.reshape((blocks, block_rows) + array.shape[1:])

    def update_block(item):
        part_state, part_queries, part_pos, part_seg, part_index = item
        return fold_block(
            part_state, part_queries, keys, values, visible_fn(part_pos, part_seg, part_index)
        )

    pieces = (
        tuple((in_blocks(member) for member in state)),
        in_blocks(queries),
        in_blocks(query_pos),
        in_blocks(query_seg),
        in_blocks(query_index),
    )
    result = lax.map(update_block, pieces)
    return tuple((member.reshape((-1,) + member.shape[2:]) for member in result))


def local(x_rows, norm_gain, w_query, w_keyval, w_out, prefix_cache, page_table, request_ids):
    tp_size = lax.axis_size("tp")
    grp_size = lax.axis_size("grp")
    tp_index = lax.axis_index("tp")
    grp_index = lax.axis_index("grp")
    tok_dev = x_rows.shape[0]
    tok_group = tok_dev * tp_size
    heads_dev = w_query.shape[1] // HD
    kv_cols = w_keyval.shape[2]
    kv_need = max(HD, HD * KVH // tp_size)
    kv_heads = kv_need // HD
    per_kv = heads_dev // kv_heads
    pages_dev = prefix_cache.shape[0]
    page_len = prefix_cache.shape[1]
    prefix_len = pages_dev * grp_size * page_len
    seg_count = 2 * grp_size
    block_rows = min(512, tok_group)
    wide = x_rows.astype(jnp.float32)
    variance = jnp.mean(wide * wide, axis=-1, keepdims=True) + 1e-05
    inverse = lax.rsqrt(variance)
    normed = (wide * inverse * norm_gain).astype(jnp.bfloat16)
    kv_weight = w_keyval.reshape(w_keyval.shape[0], 2 * kv_cols)
    piece = lax.all_gather(normed, "tp", axis=0, tiled=True)
    query_part = jnp.dot(piece, w_query, preferred_element_type=jnp.float32)
    kv_part = jnp.dot(piece, kv_weight, preferred_element_type=jnp.float32)
    projected = jnp.concatenate([query_part, kv_part], axis=1)
    query_cols = heads_dev * HD
    group_start = grp_index * tok_group
    token_index = group_start + jnp.arange(tok_group, dtype=jnp.int32)
    own_seg = lax.dynamic_slice_in_dim(request_ids, group_start, tok_group, 0)
    own_pos = prefix_len + token_index - segment_first(request_ids, own_seg, seg_count)
    queries = rotate(projected[:, :query_cols].reshape(tok_group, heads_dev, HD), own_pos).astype(
        jnp.bfloat16
    )
    queries = queries.reshape(tok_group, kv_heads, per_kv, HD)
    kv_local = projected[:, query_cols:].astype(jnp.bfloat16).reshape(tok_group, 2, kv_cols)
    cache_local = prefix_cache.reshape(pages_dev * page_len, 2, kv_cols)
    kv_own = kv_local
    cache_own = cache_local
    kv_peer, cache_peer = swapped((kv_own, cache_own), "tp", 0)
    lower = tp_index >> 0 & 1 == 0
    kv_own = join_pair(lower, kv_own, kv_peer)
    cache_own = join_pair(lower, cache_own, cache_peer)
    keys_own = rotate(
        kv_own[:, 0].reshape(tok_group, kv_heads, HD).astype(jnp.float32), own_pos
    ).astype(jnp.bfloat16)
    values_own = kv_own[:, 1].reshape(tok_group, kv_heads, HD)
    keys_prev, values_prev = shifted((keys_own, values_own), "grp", 1)
    prev_start = jnp.maximum(group_start - tok_group, 0)
    prev_index = group_start - tok_group + jnp.arange(tok_group, dtype=jnp.int32)
    prev_seg = jnp.where(
        grp_index > 0, lax.dynamic_slice_in_dim(request_ids, prev_start, tok_group, 0), -1
    )
    prev_pos = prefix_len + prev_index - segment_first(request_ids, prev_seg, seg_count)
    suffix_keys = jnp.concatenate([keys_prev, keys_own], axis=0)
    suffix_values = jnp.concatenate([values_prev, values_own], axis=0)
    suffix_seg = jnp.concatenate([prev_seg, own_seg], axis=0)
    suffix_pos = jnp.concatenate([prev_pos, own_pos], axis=0)
    suffix_index = jnp.concatenate([prev_index, token_index], axis=0)

    def suffix_visible(query_pos, query_seg, query_index):
        same = (suffix_seg[None, :] == query_seg[:, None]) & (
            suffix_index[None, :] <= query_index[:, None]
        )
        return same & (
            (query_pos[:, None] - suffix_pos[None, :] < prefix_len) | (suffix_pos[None, :] < SINKS)
        )

    start_state = (
        jnp.full((tok_group, kv_heads, per_kv), -1e30, jnp.float32),
        jnp.zeros((tok_group, kv_heads, per_kv), jnp.float32),
        jnp.zeros((tok_group, kv_heads, per_kv, HD), jnp.float32),
    )
    state = fold_all(
        start_state,
        queries,
        own_pos,
        own_seg,
        token_index,
        suffix_keys,
        suffix_values,
        suffix_visible,
        block_rows,
    )
    page_labels = jnp.arange(page_table.shape[0], dtype=jnp.int32)
    cache_keys = cache_own[:, 0].reshape(pages_dev * page_len, kv_heads, HD)
    cache_values = cache_own[:, 1].reshape(pages_dev * page_len, kv_heads, HD)
    piece_keys = lax.all_gather(cache_keys, "grp", axis=0, tiled=True)
    piece_values = lax.all_gather(cache_values, "grp", axis=0, tiled=True)
    rows = piece_keys.shape[0]
    physical = jnp.arange(rows // page_len, dtype=jnp.int32)
    logical = jnp.sum(
        jnp.where(page_table[None, :] == physical[:, None], page_labels[None, :], 0), axis=1
    )
    key_pos = (
        logical[:, None] * page_len + jnp.arange(page_len, dtype=jnp.int32)[None, :]
    ).reshape(rows)

    def prefix_visible(query_pos, query_seg, query_index):
        before = key_pos[None, :] <= query_pos[:, None]
        return before & (
            (query_pos[:, None] - key_pos[None, :] < prefix_len) | (key_pos[None, :] < SINKS)
        )

    state = fold_all(
        state,
        queries,
        own_pos,
        own_seg,
        token_index,
        piece_keys,
        piece_values,
        prefix_visible,
        block_rows,
    )
    attn = (state[2] / state[1][..., None]).reshape(tok_group, heads_dev * HD).astype(jnp.bfloat16)
    rows = attn
    return lax.psum_scatter(
        jnp.dot(rows, w_out, preferred_element_type=jnp.float32).astype(jnp.bfloat16),
        "tp",
        scatter_dimension=0,
        tiled=True,
    )


def solution(mesh):
    placed = (
        P(("grp", "tp"), None),
        P(),
        P(None, "tp"),
        P(None, None, "tp"),
        P("tp", None),
        P("grp", None, None, "tp"),
        P(),
        P(),
    )
    return jax.shard_map(
        local, mesh=mesh, in_specs=placed, out_specs=P(("grp", "tp"), None), check_vma=False
    )
```

profile of v0, /device:TPU:1, one launch (start us, length us, event | category | flops | bytes accessed | tf_op | source)
XLA Modules:
  0.0 373.4 jit_solution(2221443877971759652)
XLA Ops:
  11.0 2.6 collective-permute-start.3
  18.9 96.0 %all-gather.4.cloned.1.call-done = bf16[1024,4096]{1,0:T(8,128)(2,1)} async-done(((bf16[64,4096]{1,0:T(8,128)(2,1)}), bf16[1024,4096]{1,0:T(8,128)(2,1)}) %all-gather.4.cloned.1.call-update) | async-done | bytes 8388624 | tf_op jit(solution)/shard_map/all_gather | solution.py:118
  115.0 6.7 %convolution_convert_fusion.1 = bf16[1024,128]{0,1:T(8,128)(2,1)S(1)} fusion(bf16[1024,4096]{1,0:T(8,128)(2,1)} %all-gather.4.cloned.1.call-done, bf16[4096,128]{0,1:T(8,128)(2,1)} %bitcast.261), kind=kOutput, calls=%fused_computation.79 | convolution fusion | flops 1073872896 | bytes 9699328 | tf_op jit(solution)/shard_map/dot_general | solution.py:120
  124.2 4.7 %collective-permute-done = bf16[1024,2,64]{0,2,1:T(8,128)(2,1)S(1)} collective-permute-done((bf16[1024,2,64]{0,2,1:T(8,128)(2,1)S(1)}, bf16[1024,2,64]{0,2,1:T(8,128)(2,1)S(1)}, u32[]{:S(2)}, u32[]{:S(2)}) %collective-permute-start) | collective-permute-done | bytes 262176 | tf_op jit(solution)/shard_map/ppermute | solution.py:18
  131.0 4.5 %collective-permute-start.1 = (bf16[1024,1,128]{0,2,1:T(8,128)(2,1)}, bf16[1024,1,128]{0,2,1:T(8,128)(2,1)}, u32[]{:S(2)}, u32[]{:S(2)}) collective-permute-start(bf16[1024,1,128]{0,2,1:T(8,128)(2,1)} %pad_maximum_fusion.2), channel_id=1, source_target_pairs={{0,16},{16,32},{32,48},{48,64},{64,80},{80,96},{96,112},{112,128},... | collective-permute-start | bytes 786440 | tf_op jit(solution)/shard_map/ppermute | solution.py:24
  146.6 25.5 %while.27 = (s32[]{:T(128)}, f32[2,512,1,2]{1,3,2,0:T(2,128)S(1)}, f32[2,512,1,2]{1,3,2,0:T(2,128)S(1)}, f32[2,512,1,2,128]{4,1,3,2,0:T(8,128)}, s32[2048]{0:T(1...) while((s32[]{:T(128)}, f32[2,512,1,2]{1,3,2,0:T(2,128)S(1)}, ...), condition=%wide.region_8.9_spmd, body=%wide.region_5.8_spmd.sunk | while | flops 1108483072 | bytes 39688408 | solution.py:92
  148.8 3.2 fusion.107
  152.1 2.9 fusion.108
  155.0 3.4 fusion.110
  161.6 3.2 fusion.107
  164.8 2.9 fusion.108
  167.7 3.4 fusion.110
  172.1 45.6 %all-gather.8.cloned.1.call-done = bf16[4096,1,128]{2,0,1:T(8,128)(2,1)} async-done(((bf16[256,1,128]{2,0,1:T(8,128)(2,1)}), bf16[4096,1,128]{2,0,1:T(8,128)(2,1)}) %all-gather.8.cloned.1.call-update) | async-done | bytes 1048592 | tf_op jit(solution)/shard_map/all_gather | solution.py:184
  217.7 41.1 %while.28 = (s32[]{:T(128)}, f32[2,512,1,2]{1,3,2,0:T(2,128)S(1)}, f32[2,512,1,2,128]{4,3,1,0,2:T(2,128)}, f32[2,512,1,2]{1,3,2,0:T(2,128)S(1)}, f32[2,512,1,2]{...) while((s32[]{:T(128)}, f32[2,512,1,2]{1,3,2,0:T(2,128)S(1)}, ...), condition=%wide.region_13.14_spmd.clone, body=%wide.region_10.13_spmd.clone.sunk | while | flops 2212773888 | bytes 71670216 | solution.py:92
  217.9 2.6 fusion.113
  220.5 5.1 %fusion.114 = (f32[512,2]{0,1:T(2,128)S(1)}, f32[512,2,4096]{2,0,1:T(8,128)S(1)}) fusion(pred[512,4096]{1,0:T(8,128)(4,1)S(1)} %fusion.113, bf16[4096,1,128]{2,0,1:T(8,128)(2,1)} %get-tuple-element.555, bf16[2,512,1,2,128]{4,1,3,2,0:T(8,128)(2,1)} %get-tuple-element.554, s32[]{:T(128)S(6)} %copy.72), kind=kOutput, calls=%fused_computation.39.clone.1 | convolution fusion | flops 1086323712 | bytes 20189188 | tf_op jit(solution)/shard_map/while/body/eval_jaxpr/qgrd,kgd->qgrk/dot_general | solution.py:56
  225.7 5.3 %fusion.116 = f32[512,2]{0,1:T(2,128)S(1)} fusion(f32[512,2,4096]{2,0,1:T(8,128)S(1)} %get-tuple-element.478, f32[512,2]{0,1:T(2,128)S(1)} %get-tuple-element.480, pred[512,4096]{1,0:T(8,128)(4,1)S(1)} %fusion.113), kind=kLoop, calls=%fused_computation.41.clone.1 | loop fusion | flops 20970496 | bytes 18882560 | tf_op jit(solution)/shard_map/while/body/eval_jaxpr/reduce_sum | solution.py:64
  231.0 6.0 %fusion.118 = f32[1,512,1,2,128]{4,1,3,2,0:T(8,128)S(1)} fusion(f32[512,2,4096]{2,0,1:T(8,128)S(1)} %get-tuple-element.478, f32[512,2]{0,1:T(2,128)S(1)} %get-tuple-element.480, pred[512,4096]{1,0:T(8,128)(4,1)S(1)} %fusion.113, bf16[4096,1,128]{2,0,1:T(8,128)(2,1)S(1)} %copy-done.3, f32[2,512,1,2,128]{4,1,3,2,0:T(8,128)S(1)} %copy-done.6, ...), kind=kOutput, calls=%fused_computation.50.clone.1 | convolution fusion | flops 1094975488 | bytes 20979716 | tf_op jit(solution)/shard_map/while/body/eval_jaxpr/qgrk,kgd->qgrd/dot_general | solution.py:65
  238.4 2.6 fusion.113
  241.0 5.1 %fusion.114 = (f32[512,2]{0,1:T(2,128)S(1)}, f32[512,2,4096]{2,0,1:T(8,128)S(1)}) fusion(pred[512,4096]{1,0:T(8,128)(4,1)S(1)} %fusion.113, bf16[4096,1,128]{2,0,1:T(8,128)(2,1)} %get-tuple-element.555, bf16[2,512,1,2,128]{4,1,3,2,0:T(8,128)(2,1)} %get-tuple-element.554, s32[]{:T(128)S(6)} %copy.72), kind=kOutput, calls=%fused_computation.39.clone.1 | convolution fusion | flops 1086323712 | bytes 20189188 | tf_op jit(solution)/shard_map/while/body/eval_jaxpr/qgrd,kgd->qgrk/dot_general | solution.py:56
  246.2 5.3 %fusion.116 = f32[512,2]{0,1:T(2,128)S(1)} fusion(f32[512,2,4096]{2,0,1:T(8,128)S(1)} %get-tuple-element.478, f32[512,2]{0,1:T(2,128)S(1)} %get-tuple-element.480, pred[512,4096]{1,0:T(8,128)(4,1)S(1)} %fusion.113), kind=kLoop, calls=%fused_computation.41.clone.1 | loop fusion | flops 20970496 | bytes 18882560 | tf_op jit(solution)/shard_map/while/body/eval_jaxpr/reduce_sum | solution.py:64
  251.5 6.0 %fusion.118 = f32[1,512,1,2,128]{4,1,3,2,0:T(8,128)S(1)} fusion(f32[512,2,4096]{2,0,1:T(8,128)S(1)} %get-tuple-element.478, f32[512,2]{0,1:T(2,128)S(1)} %get-tuple-element.480, pred[512,4096]{1,0:T(8,128)(4,1)S(1)} %fusion.113, bf16[4096,1,128]{2,0,1:T(8,128)(2,1)S(1)} %copy-done.3, f32[2,512,1,2,128]{4,1,3,2,0:T(8,128)S(1)} %copy-done.6, ...), kind=kOutput, calls=%fused_computation.50.clone.1 | convolution fusion | flops 1094975488 | bytes 20979716 | tf_op jit(solution)/shard_map/while/body/eval_jaxpr/qgrk,kgd->qgrd/dot_general | solution.py:65
  260.2 6.8 %convolution_convert_fusion = bf16[1024,4096]{1,0:T(8,128)(2,1)} fusion(bf16[256,4096]{1,0:T(8,128)(2,1)S(1)} %copy-done, f32[128,8,2,128]{3,2,1,0:T(2,128)S(1)} %bitcast.248, f32[128,8,2,128]{3,2,1,0:T(2,128)} %bitcast.249), kind=kOutput, calls=%fused_computation.74 | convolution fusion | flops 2152202240 | bytes 12582912 | tf_op jit(solution)/shard_map/dot_general | solution.py:214
  267.1 99.8 %reduce-scatter.2.cloned.1.call-done = bf16[64,4096]{1,0:T(8,128)(2,1)} async-done(((bf16[1024,4096]{1,0:T(8,128)(2,1)}), bf16[64,4096]{1,0:T(8,128)(2,1)}) %reduce-scatter.2.cloned.1.call-update) | async-done | bytes 524304 | tf_op jit(solution)/shard_map/reduce_scatter | solution.py:213
  (108 shorter events, 35.9 us)
Async XLA Ops:
  6.5 253.7 %copy-start = (bf16[256,4096]{1,0:T(8,128)(2,1)S(1)}, bf16[256,4096]{1,0:T(8,128)(2,1)}, u32[]{:S(2)}) copy-start(bf16[256,4096]{1,0:T(8,128)(2,1)} %param.16) | copy-start | bytes 6291460
  6.5 108.4 %all-gather.4.cloned.1.call-start = ((), (), s32[]{:S(2)}) async-start(), calls=%async_computation.1 | async-start | bytes 8912896 | tf_op jit(solution)/shard_map/all_gather | solution.py:118
  10.0 162.1 %all-gather.6.cloned.1.call-start = ((), (), s32[]{:S(2)}) async-start(), calls=%async_computation.2 | async-start | bytes 1114112 | tf_op jit(solution)/shard_map/all_gather | solution.py:183
  11.0 4.9 %collective-permute-start.3 = (bf16[256,2,64]{2,0,1:T(8,128)(2,1)S(1)}, bf16[256,2,64]{2,0,1:T(8,128)(2,1)S(1)}, u32[]{:S(2)}, u32[]{:S(2)}) collective-permute-start(bf16[256,2,64]{2,0,1:T(8,128)(2,1)S(1)} %bitcast.251), channel_id=1, source_target_pairs={{0,1},{1,0},{2,3},{3,2},{4,5},{5,4},{6,7},{7,6},{8,9},{9,8},{10,11... | collective-permute-start | bytes 196616 | tf_op jit(solution)/shard_map/ppermute | solution.py:18
  16.8 200.9 %all-gather.8.cloned.1.call-start = ((), (), s32[]{:S(2)}) async-start(), calls=%async_computation.3 | async-start | bytes 1114112 | tf_op jit(solution)/shard_map/all_gather | solution.py:184
  18.9 348.0 %reduce-scatter.2.cloned.1.call-start = ((), (), s32[]{:S(2)}) async-start(), calls=%async_computation.4 | async-start | bytes 8912896 | tf_op jit(solution)/shard_map/reduce_scatter | solution.py:213
  115.0 6.8 %copy-start.1 = (bf16[1024,4096]{1,0:T(8,128)(2,1)S(1)}, bf16[1024,4096]{1,0:T(8,128)(2,1)}, u32[]{:S(2)}) copy-start(bf16[1024,4096]{1,0:T(8,128)(2,1)} %all-gather.4.cloned.1.call-done) | copy-start | bytes 25165828
  115.0 6.8 %copy-start.2 = (bf16[4096,256]{1,0:T(8,128)(2,1)S(1)}, bf16[4096,256]{1,0:T(8,128)(2,1)}, u32[]{:S(2)}) copy-start(bf16[4096,256]{1,0:T(8,128)(2,1)} %param.14) | copy-start | bytes 6291460
  121.6 7.3 %collective-permute-start = (bf16[1024,2,64]{0,2,1:T(8,128)(2,1)S(1)}, bf16[1024,2,64]{0,2,1:T(8,128)(2,1)S(1)}, u32[]{:S(2)}, u32[]{:S(2)}) collective-permute-start(bf16[1024,2,64]{0,2,1:T(8,128)(2,1)S(1)} %bitcast.253), channel_id=1, source_target_pairs={{0,1},{1,0},{2,3},{3,2},{4,5},{5,4},{6,7},{7,6},{8,9},{9,8},{10,11... | collective-permute-start | bytes 786440 | tf_op jit(solution)/shard_map/ppermute | solution.py:18
  131.0 12.3 %collective-permute-start.1 = (bf16[1024,1,128]{0,2,1:T(8,128)(2,1)}, bf16[1024,1,128]{0,2,1:T(8,128)(2,1)}, u32[]{:S(2)}, u32[]{:S(2)}) collective-permute-start(bf16[1024,1,128]{0,2,1:T(8,128)(2,1)} %pad_maximum_fusion.2), channel_id=1, source_target_pairs={{0,16},{16,32},{32,48},{48,64},{64,80},{80,96},{96,112},{112,128},... | collective-permute-start | bytes 786440 | tf_op jit(solution)/shard_map/ppermute | solution.py:24
  138.4 6.9 %collective-permute-start.2 = (bf16[1024,1,128]{0,2,1:T(8,128)(2,1)S(1)}, bf16[1024,1,128]{0,2,1:T(8,128)(2,1)}, u32[]{:S(2)}, u32[]{:S(2)}) collective-permute-start(bf16[1024,1,128]{0,2,1:T(8,128)(2,1)S(1)} %get-tuple-element.302), channel_id=1, source_target_pairs={{0,16},{16,32},{32,48},{48,64},{64,80},{80,96},{96,112},{112,128},... | collective-permute-start | bytes 786440 | tf_op jit(solution)/shard_map/ppermute | solution.py:24
  148.8 6.2 %copy-start.4 = (f32[2,512,1,2,128]{4,1,3,2,0:T(8,128)S(1)}, f32[2,512,1,2,128]{4,1,3,2,0:T(8,128)}, u32[]{:S(2)}) copy-start(f32[2,512,1,2,128]{4,1,3,2,0:T(8,128)} %get-tuple-element.499) | copy-start | bytes 3145732 | tf_op jit(solution)/shard_map/while
  158.4 1.0 copy-start.5
  161.6 6.2 %copy-start.4 = (f32[2,512,1,2,128]{4,1,3,2,0:T(8,128)S(1)}, f32[2,512,1,2,128]{4,1,3,2,0:T(8,128)}, u32[]{:S(2)}) copy-start(f32[2,512,1,2,128]{4,1,3,2,0:T(8,128)} %get-tuple-element.499) | copy-start | bytes 3145732 | tf_op jit(solution)/shard_map/while
  171.1 1.0 copy-start.5
  225.7 5.3 %copy-start.3 = (bf16[4096,1,128]{2,0,1:T(8,128)(2,1)S(1)}, bf16[4096,1,128]{2,0,1:T(8,128)(2,1)}, u32[]{:S(2)}) copy-start(bf16[4096,1,128]{2,0,1:T(8,128)(2,1)} %get-tuple-element.557) | copy-start | bytes 3145732 | tf_op jit(solution)/shard_map/while
  225.7 5.3 %copy-start.6 = (f32[2,512,1,2,128]{4,1,3,2,0:T(8,128)S(1)}, f32[2,512,1,2,128]{4,1,3,2,0:T(8,128)}, u32[]{:S(2)}) copy-start(f32[2,512,1,2,128]{4,1,3,2,0:T(8,128)} %get-tuple-element.556) | copy-start | bytes 3145732 | tf_op jit(solution)/shard_map/while
  246.2 5.3 %copy-start.3 = (bf16[4096,1,128]{2,0,1:T(8,128)(2,1)S(1)}, bf16[4096,1,128]{2,0,1:T(8,128)(2,1)}, u32[]{:S(2)}) copy-start(bf16[4096,1,128]{2,0,1:T(8,128)(2,1)} %get-tuple-element.557) | copy-start | bytes 3145732 | tf_op jit(solution)/shard_map/while
  246.2 5.3 %copy-start.6 = (f32[2,512,1,2,128]{4,1,3,2,0:T(8,128)S(1)}, f32[2,512,1,2,128]{4,1,3,2,0:T(8,128)}, u32[]{:S(2)}) copy-start(f32[2,512,1,2,128]{4,1,3,2,0:T(8,128)} %get-tuple-element.556) | copy-start | bytes 3145732 | tf_op jit(solution)/shard_map/while
Sparse Core Ops, SparseCore 0:
  10.1 104.8 all-gather.3
  117.7 48.2 all-gather.5
  168.7 48.9 all-gather.7
  267.2 99.6 reduce-scatter.1
where the time goes:
time: 374 us; the launch traced here: 373 us
  waiting for transfers between devices  246 us (66%)
  matrix products  51.4 us (14%)
  other arithmetic  40.5 us (11%)
  between operations  13.4 us (4%)
  local copies, waits for them, and re-layouts  12.1 us (3%)
  starting transfers between devices  9.4 us (3%)
    reduce_scatter x1, waiting for transfers between devices, local(): lax.psum_scatter(jnp.dot(rows, w_out, preferred_element_type=jnp.float32)...  99.8 us
    all_gather x1, waiting for transfers between devices, local(): piece = lax.all_gather(normed, 'tp', axis=0, tiled=True)  96 us
    all_gather x1, waiting for transfers between devices, local(): piece_values = lax.all_gather(cache_values, 'grp', axis=0, tiled=True)  45.6 us
    dot_general x4, matrix products, fold_block(): jnp.einsum('qgrk,kgd->qgrd', weights.astype(jnp.bfloat16), values, prefer...  18.8 us
    dot_general x4, matrix products, fold_block(): jnp.einsum('qgrd,kgd->qgrk', queries, keys, preferred_element_type=jnp.fl...  16.7 us
    reduce_sum x4, other arithmetic, fold_block(): new_sum = run_sum * factor + jnp.sum(weights, axis=-1)  16.3 us
  transfers between devices with their start and end apart: 8, of which 5 were waited for; matrix products, arithmetic and copies ran while one was open for 13% of the time, Pallas kernels for 0%

commit v1 on v0

--- a/solution.py
+++ b/solution.py
@@ -115,7 +115,9 @@
     inverse = lax.rsqrt(variance)
     normed = (wide * inverse * norm_gain).astype(jnp.bfloat16)
     kv_weight = w_keyval.reshape(w_keyval.shape[0], 2 * kv_cols)
-    piece = lax.all_gather(normed, "tp", axis=0, tiled=True)
+    piece = jnp.concatenate(
+        lax.all_to_all(jnp.stack([normed] * lax.axis_size("tp")), "tp", 0, 0), axis=0
+    )
     query_part = jnp.dot(piece, w_query, preferred_element_type=jnp.float32)
     kv_part = jnp.dot(piece, kv_weight, preferred_element_type=jnp.float32)
     projected = jnp.concatenate([query_part, kv_part], axis=1)

time: 374 us -> 477 us (1.28)
  waiting for transfers between devices: 246 us -> 329 us
  starting transfers between devices: 9.4 us -> 21 us
  local copies, waits for them, and re-layouts: 12.1 us -> 20.2 us
    ppermute x2, waiting for transfers between devices: 4.8 us -> 186 us  [swapped(): return lax.ppermute(block, axis, route)]
    all_gather x1 -> x0, waiting for transfers between devices: 96 us -> none  [local(): piece = lax.all_gather(normed, 'tp', axis=0, tiled=True)]
    all_to_all x0 -> x1, starting transfers between devices: none -> 10.3 us  [local(): lax.all_to_all(jnp.stack([normed] * lax.axis_size('tp')), 'tp', 0, 0)]
  transfers between devices with their start and end apart: 8 -> 8, of which waited for: 5 -> 4; matrix products, arithmetic and copies ran while one was open for 13% -> 11% of each run, Pallas kernels for 0% -> 0%
where the time goes in v1:
time: 477 us
  waiting for transfers between devices  329 us (69%)
  matrix products  54.7 us (11%)
  other arithmetic  37.7 us (8%)
  starting transfers between devices  21 us (4%)
  local copies, waits for them, and re-layouts  20.2 us (4%)
  between operations  13.4 us (3%)
    ppermute x2, waiting for transfers between devices, swapped(): return lax.ppermute(block, axis, route)  186 us
    reduce_scatter x1, waiting for transfers between devices, local(): lax.psum_scatter(jnp.dot(rows, w_out, preferred_element_type=jnp.float32)...  99.8 us
    all_gather x1, waiting for transfers between devices, local(): piece_values = lax.all_gather(cache_values, 'grp', axis=0, tiled=True)  42.6 us
    dot_general x4, matrix products, fold_block(): jnp.einsum('qgrk,kgd->qgrd', weights.astype(jnp.bfloat16), values, prefer...  18.7 us
    dot_general x4, matrix products, fold_block(): jnp.einsum('qgrd,kgd->qgrk', queries, keys, preferred_element_type=jnp.fl...  16.5 us
    reduce_sum x4, other arithmetic, fold_block(): new_sum = run_sum * factor + jnp.sum(weights, axis=-1)  16.3 us
    all_to_all x1, starting transfers between devices, local(): lax.all_to_all(jnp.stack([normed] * lax.axis_size('tp')), 'tp', 0, 0)  10.3 us
  transfers between devices with their start and end apart: 8, of which 4 were waited for; matrix products, arithmetic and copies ran while one was open for 11% of the time, Pallas kernels for 0%

profile of v1, /device:TPU:1, one launch (start us, length us, event | category | flops | bytes accessed | tf_op | source)
XLA Modules:
  0.0 476.7 jit_solution(3717066883120584008)
XLA Ops:
  9.2 4.3 stack.2
  13.5 10.3 %all-to-all-start = ((bf16[16,64,4096]{2,1,0:T(8,128)(2,1)}), bf16[16,64,4096]{2,1,0:T(8,128)(2,1)}, u32[]{:S(2)}, u32[]{:S(2)}) async-start(bf16[16,64,4096]{2,1,0:T(8,128)(2,1)} %stack.2), calls=%async_computation | async-start | bytes 16777216 | tf_op jit(solution)/shard_map/all_to_all | solution.py:119
  26.1 185.8 %collective-permute-done.3 = bf16[256,2,64]{2,0,1:T(8,128)(2,1)S(1)} collective-permute-done((bf16[256,2,64]{2,0,1:T(8,128)(2,1)S(1)}, bf16[256,2,64]{2,0,1:T(8,128)(2,1)S(1)}, u32[]{:S(2)}, u32[]{:S(2)}) %collective-permute-start.3) | collective-permute-done | bytes 65568 | tf_op jit(solution)/shard_map/ppermute | solution.py:18
  213.0 4.2 copy.46
  218.4 6.7 %convolution_convert_fusion.1 = bf16[1024,128]{0,1:T(8,128)(2,1)S(1)} fusion(bf16[1024,4096]{1,0:T(8,128)(2,1)} %bitcast.19, bf16[4096,128]{0,1:T(8,128)(2,1)} %bitcast.266), kind=kOutput, calls=%fused_computation.79 | convolution fusion | flops 1073872896 | bytes 9699328 | tf_op jit(solution)/shard_map/dot_general | solution.py:122
  227.4 6.1 %fusion.83 = f32[1024,2,128]{0,2,1:T(8,128)S(1)} fusion(bf16[1024,4096,1]{1,0,2:T(8,128)(2,1)} %bitcast.20, bf16[2,128,4096]{2,1,0:T(8,128)(2,1)S(1)} %bitcast.254), kind=kOutput, calls=%fused_computation.128 | convolution fusion | flops 2147483648 | bytes 11534336 | tf_op jit(solution)/shard_map/dot_general | solution.py:121
  236.3 4.8 %collective-permute-start.1 = (bf16[1024,1,128]{0,2,1:T(8,128)(2,1)}, bf16[1024,1,128]{0,2,1:T(8,128)(2,1)}, u32[]{:S(2)}, u32[]{:S(2)}) collective-permute-start(bf16[1024,1,128]{0,2,1:T(8,128)(2,1)} %pad_maximum_fusion.2), channel_id=1, source_target_pairs={{0,16},{16,32},{32,48},{48,64},{64,80},{80,96},{96,112},{112,128},... | collective-permute-start | bytes 786440 | tf_op jit(solution)/shard_map/ppermute | solution.py:24
  253.2 25.2 %while.27 = (s32[]{:T(128)}, f32[2,512,1,2]{1,3,2,0:T(2,128)S(1)}, f32[2,512,1,2]{1,3,2,0:T(2,128)S(1)}, f32[2,512,1,2,128]{4,1,3,2,0:T(8,128)}, s32[2048]{0:T(1...) while((s32[]{:T(128)}, f32[2,512,1,2]{1,3,2,0:T(2,128)S(1)}, ...), condition=%wide.region_8.9_spmd, body=%wide.region_5.8_spmd.sunk | while | flops 1108483072 | bytes 41785588 | solution.py:92
  255.4 3.1 fusion.107
  258.5 2.9 fusion.108
  261.4 3.4 fusion.110
  268.0 3.1 fusion.107
  271.1 2.9 fusion.108
  274.1 3.4 fusion.110
  278.4 42.6 %all-gather.5.cloned.1.call-done = bf16[4096,1,128]{2,0,1:T(8,128)(2,1)} async-done(((bf16[256,1,128]{2,0,1:T(8,128)(2,1)}), bf16[4096,1,128]{2,0,1:T(8,128)(2,1)}) %all-gather.5.cloned.1.call-update) | async-done | bytes 1048592 | tf_op jit(solution)/shard_map/all_gather | solution.py:186
  321.0 41.1 %while.28 = (s32[]{:T(128)}, f32[2,512,1,2]{1,3,2,0:T(2,128)S(1)}, f32[2,512,1,2,128]{4,3,1,0,2:T(2,128)}, f32[2,512,1,2]{1,3,2,0:T(2,128)S(1)}, f32[2,512,1,2]{...) while((s32[]{:T(128)}, f32[2,512,1,2]{1,3,2,0:T(2,128)S(1)}, ...), condition=%wide.region_13.14_spmd.clone, body=%wide.region_10.13_spmd.clone.sunk | while | flops 2212773888 | bytes 71670216 | solution.py:92
  323.8 5.1 %fusion.114 = (f32[512,2]{0,1:T(2,128)S(1)}, f32[512,2,4096]{2,0,1:T(8,128)S(1)}) fusion(pred[512,4096]{1,0:T(8,128)(4,1)S(1)} %fusion.113, bf16[4096,1,128]{2,0,1:T(8,128)(2,1)} %get-tuple-element.496, bf16[2,512,1,2,128]{4,1,3,2,0:T(8,128)(2,1)} %get-tuple-element.495, s32[]{:T(128)S(6)} %copy.79), kind=kOutput, calls=%fused_computation.39.clone.1 | convolution fusion | flops 1086323712 | bytes 20189188 | tf_op jit(solution)/shard_map/while/body/eval_jaxpr/qgrd,kgd->qgrk/dot_general | solution.py:56
  329.0 5.3 %fusion.116 = f32[512,2]{0,1:T(2,128)S(1)} fusion(f32[512,2,4096]{2,0,1:T(8,128)S(1)} %get-tuple-element.419, f32[512,2]{0,1:T(2,128)S(1)} %get-tuple-element.421, pred[512,4096]{1,0:T(8,128)(4,1)S(1)} %fusion.113), kind=kLoop, calls=%fused_computation.41.clone.1 | loop fusion | flops 20970496 | bytes 18882560 | tf_op jit(solution)/shard_map/while/body/eval_jaxpr/reduce_sum | solution.py:64
  334.3 6.0 %fusion.118 = f32[1,512,1,2,128]{4,1,3,2,0:T(8,128)S(1)} fusion(f32[512,2,4096]{2,0,1:T(8,128)S(1)} %get-tuple-element.419, f32[512,2]{0,1:T(2,128)S(1)} %get-tuple-element.421, pred[512,4096]{1,0:T(8,128)(4,1)S(1)} %fusion.113, bf16[4096,1,128]{2,0,1:T(8,128)(2,1)S(1)} %copy-done.5, f32[2,512,1,2,128]{4,1,3,2,0:T(8,128)S(1)} %copy-done.9, ...), kind=kOutput, calls=%fused_computation.50.clone.1 | convolution fusion | flops 1094975488 | bytes 20979716 | tf_op jit(solution)/shard_map/while/body/eval_jaxpr/qgrk,kgd->qgrd/dot_general | solution.py:65
  344.3 5.1 %fusion.114 = (f32[512,2]{0,1:T(2,128)S(1)}, f32[512,2,4096]{2,0,1:T(8,128)S(1)}) fusion(pred[512,4096]{1,0:T(8,128)(4,1)S(1)} %fusion.113, bf16[4096,1,128]{2,0,1:T(8,128)(2,1)} %get-tuple-element.496, bf16[2,512,1,2,128]{4,1,3,2,0:T(8,128)(2,1)} %get-tuple-element.495, s32[]{:T(128)S(6)} %copy.79), kind=kOutput, calls=%fused_computation.39.clone.1 | convolution fusion | flops 1086323712 | bytes 20189188 | tf_op jit(solution)/shard_map/while/body/eval_jaxpr/qgrd,kgd->qgrk/dot_general | solution.py:56
  349.5 5.3 %fusion.116 = f32[512,2]{0,1:T(2,128)S(1)} fusion(f32[512,2,4096]{2,0,1:T(8,128)S(1)} %get-tuple-element.419, f32[512,2]{0,1:T(2,128)S(1)} %get-tuple-element.421, pred[512,4096]{1,0:T(8,128)(4,1)S(1)} %fusion.113), kind=kLoop, calls=%fused_computation.41.clone.1 | loop fusion | flops 20970496 | bytes 18882560 | tf_op jit(solution)/shard_map/while/body/eval_jaxpr/reduce_sum | solution.py:64
  354.8 6.0 %fusion.118 = f32[1,512,1,2,128]{4,1,3,2,0:T(8,128)S(1)} fusion(f32[512,2,4096]{2,0,1:T(8,128)S(1)} %get-tuple-element.419, f32[512,2]{0,1:T(2,128)S(1)} %get-tuple-element.421, pred[512,4096]{1,0:T(8,128)(4,1)S(1)} %fusion.113, bf16[4096,1,128]{2,0,1:T(8,128)(2,1)S(1)} %copy-done.5, f32[2,512,1,2,128]{4,1,3,2,0:T(8,128)S(1)} %copy-done.9, ...), kind=kOutput, calls=%fused_computation.50.clone.1 | convolution fusion | flops 1094975488 | bytes 20979716 | tf_op jit(solution)/shard_map/while/body/eval_jaxpr/qgrk,kgd->qgrd/dot_general | solution.py:65
  363.5 6.8 %convolution_convert_fusion = bf16[1024,4096]{1,0:T(8,128)(2,1)} fusion(bf16[256,4096]{1,0:T(8,128)(2,1)S(1)} %copy-done, f32[128,8,2,128]{3,2,1,0:T(2,128)S(1)} %bitcast.252, f32[128,8,2,128]{3,2,1,0:T(2,128)} %bitcast.255), kind=kOutput, calls=%fused_computation.74 | convolution fusion | flops 2152202240 | bytes 12582912 | tf_op jit(solution)/shard_map/dot_general | solution.py:216
  370.4 99.8 %reduce-scatter.2.cloned.1.call-done = bf16[64,4096]{1,0:T(8,128)(2,1)} async-done(((bf16[1024,4096]{1,0:T(8,128)(2,1)}), bf16[64,4096]{1,0:T(8,128)(2,1)}) %reduce-scatter.2.cloned.1.call-update) | async-done | bytes 524304 | tf_op jit(solution)/shard_map/reduce_scatter | solution.py:215
  (118 shorter events, 40.2 us)
Async XLA Ops:
  6.5 357.0 %copy-start = (bf16[256,4096]{1,0:T(8,128)(2,1)S(1)}, bf16[256,4096]{1,0:T(8,128)(2,1)}, u32[]{:S(2)}) copy-start(bf16[256,4096]{1,0:T(8,128)(2,1)} %param.16) | copy-start | bytes 6291460
  13.5 10.4 %copy-start.4 = (bf16[2,128,2,64]{1,3,2,0:T(8,128)(2,1)S(1)}, bf16[2,128,2,64]{1,3,2,0:T(8,128)(2,1)}, u32[]{:S(2)}) copy-start(bf16[2,128,2,64]{1,3,2,0:T(8,128)(2,1)} %param.17) | copy-start | bytes 196612
  13.5 11.9 %copy-start.3 = (s32[16384]{0:T(1024)S(1)}, s32[16384]{0:T(1024)}, u32[]{:S(2)}) copy-start(s32[16384]{0:T(1024)} %param.19) | copy-start | bytes 196612
  13.5 203.8 %copy-start.6 = (s32[32]{0:T(128)S(1)}, s32[32]{0:T(128)}, u32[]{:S(2)}) copy-start(s32[32]{0:T(128)} %param.18) | copy-start | bytes 388
  13.5 205.0 %all-to-all-start = ((bf16[16,64,4096]{2,1,0:T(8,128)(2,1)}), bf16[16,64,4096]{2,1,0:T(8,128)(2,1)}, u32[]{:S(2)}, u32[]{:S(2)}) async-start(bf16[16,64,4096]{2,1,0:T(8,128)(2,1)} %stack.2), calls=%async_computation | async-start | bytes 16777216 | tf_op jit(solution)/shard_map/all_to_all | solution.py:119
  23.8 254.6 %all-gather.3.cloned.1.call-start = ((), (), s32[]{:S(2)}) async-start(), calls=%async_computation.2 | async-start | bytes 1114112 | tf_op jit(solution)/shard_map/all_gather | solution.py:185
  24.0 187.9 %collective-permute-start.3 = (bf16[256,2,64]{2,0,1:T(8,128)(2,1)S(1)}, bf16[256,2,64]{2,0,1:T(8,128)(2,1)S(1)}, u32[]{:S(2)}, u32[]{:S(2)}) collective-permute-start(bf16[256,2,64]{2,0,1:T(8,128)(2,1)S(1)} %bitcast.256), channel_id=1, source_target_pairs={{0,1},{1,0},{2,3},{3,2},{4,5},{5,4},{6,7},{7,6},{8,9},{9,8},{10,11... | collective-permute-start | bytes 196616 | tf_op jit(solution)/shard_map/ppermute | solution.py:18
  212.7 108.3 %all-gather.5.cloned.1.call-start = ((), (), s32[]{:S(2)}) async-start(), calls=%async_computation.3 | async-start | bytes 1114112 | tf_op jit(solution)/shard_map/all_gather | solution.py:186
  218.4 251.8 %reduce-scatter.2.cloned.1.call-start = ((), (), s32[]{:S(2)}) async-start(), calls=%async_computation.4 | async-start | bytes 8912896 | tf_op jit(solution)/shard_map/reduce_scatter | solution.py:215
  218.4 9.0 %copy-start.1 = (bf16[256,4096]{1,0:T(8,128)(2,1)S(1)}, bf16[256,4096]{1,0:T(8,128)(2,1)}, u32[]{:S(2)}) copy-start(bf16[256,4096]{1,0:T(8,128)(2,1)} %copy.46) | copy-start | bytes 6291460
  225.1 8.4 %collective-permute-start = (bf16[1024,2,64]{0,2,1:T(8,128)(2,1)S(1)}, bf16[1024,2,64]{0,2,1:T(8,128)(2,1)S(1)}, u32[]{:S(2)}, u32[]{:S(2)}) collective-permute-start(bf16[1024,2,64]{0,2,1:T(8,128)(2,1)S(1)} %bitcast.258), channel_id=1, source_target_pairs={{0,1},{1,0},{2,3},{3,2},{4,5},{5,4},{6,7},{7,6},{8,9},{9,8},{10,11... | collective-permute-start | bytes 786440 | tf_op jit(solution)/shard_map/ppermute | solution.py:18
  236.3 12.5 %collective-permute-start.1 = (bf16[1024,1,128]{0,2,1:T(8,128)(2,1)}, bf16[1024,1,128]{0,2,1:T(8,128)(2,1)}, u32[]{:S(2)}, u32[]{:S(2)}) collective-permute-start(bf16[1024,1,128]{0,2,1:T(8,128)(2,1)} %pad_maximum_fusion.2), channel_id=1, source_target_pairs={{0,16},{16,32},{32,48},{48,64},{64,80},{80,96},{96,112},{112,128},... | collective-permute-start | bytes 786440 | tf_op jit(solution)/shard_map/ppermute | solution.py:24
  245.6 5.5 %collective-permute-start.2 = (bf16[1024,1,128]{0,2,1:T(8,128)(2,1)}, bf16[1024,1,128]{0,2,1:T(8,128)(2,1)}, u32[]{:S(2)}, u32[]{:S(2)}) collective-permute-start(bf16[1024,1,128]{0,2,1:T(8,128)(2,1)} %get-tuple-element.243), channel_id=1, source_target_pairs={{0,16},{16,32},{32,48},{48,64},{64,80},{80,96},{96,112},{112,128},... | collective-permute-start | bytes 786440 | tf_op jit(solution)/shard_map/ppermute | solution.py:24
  255.4 6.0 %copy-start.2 = (bf16[2048,1,128]{2,0,1:T(8,128)(2,1)S(1)}, bf16[2048,1,128]{2,0,1:T(8,128)(2,1)}, u32[]{:S(2)}) copy-start(bf16[2048,1,128]{2,0,1:T(8,128)(2,1)} %get-tuple-element.463) | copy-start | bytes 1572868 | tf_op jit(solution)/shard_map/while
  255.4 6.0 %copy-start.7 = (f32[2,512,1,2,128]{4,1,3,2,0:T(8,128)S(1)}, f32[2,512,1,2,128]{4,1,3,2,0:T(8,128)}, u32[]{:S(2)}) copy-start(f32[2,512,1,2,128]{4,1,3,2,0:T(8,128)} %get-tuple-element.440) | copy-start | bytes 3145732 | tf_op jit(solution)/shard_map/while
  264.8 1.0 copy-start.8
  268.0 6.0 %copy-start.2 = (bf16[2048,1,128]{2,0,1:T(8,128)(2,1)S(1)}, bf16[2048,1,128]{2,0,1:T(8,128)(2,1)}, u32[]{:S(2)}) copy-start(bf16[2048,1,128]{2,0,1:T(8,128)(2,1)} %get-tuple-element.463) | copy-start | bytes 1572868 | tf_op jit(solution)/shard_map/while
  268.0 6.0 %copy-start.7 = (f32[2,512,1,2,128]{4,1,3,2,0:T(8,128)S(1)}, f32[2,512,1,2,128]{4,1,3,2,0:T(8,128)}, u32[]{:S(2)}) copy-start(f32[2,512,1,2,128]{4,1,3,2,0:T(8,128)} %get-tuple-element.440) | copy-start | bytes 3145732 | tf_op jit(solution)/shard_map/while
  277.4 1.0 copy-start.8
  329.0 5.3 %copy-start.5 = (bf16[4096,1,128]{2,0,1:T(8,128)(2,1)S(1)}, bf16[4096,1,128]{2,0,1:T(8,128)(2,1)}, u32[]{:S(2)}) copy-start(bf16[4096,1,128]{2,0,1:T(8,128)(2,1)} %get-tuple-element.498) | copy-start | bytes 3145732 | tf_op jit(solution)/shard_map/while
  329.0 5.3 %copy-start.9 = (f32[2,512,1,2,128]{4,1,3,2,0:T(8,128)S(1)}, f32[2,512,1,2,128]{4,1,3,2,0:T(8,128)}, u32[]{:S(2)}) copy-start(f32[2,512,1,2,128]{4,1,3,2,0:T(8,128)} %get-tuple-element.497) | copy-start | bytes 3145732 | tf_op jit(solution)/shard_map/while
  349.5 5.3 %copy-start.5 = (bf16[4096,1,128]{2,0,1:T(8,128)(2,1)S(1)}, bf16[4096,1,128]{2,0,1:T(8,128)(2,1)}, u32[]{:S(2)}) copy-start(bf16[4096,1,128]{2,0,1:T(8,128)(2,1)} %get-tuple-element.498) | copy-start | bytes 3145732 | tf_op jit(solution)/shard_map/while
  349.5 5.3 %copy-start.9 = (f32[2,512,1,2,128]{4,1,3,2,0:T(8,128)S(1)}, f32[2,512,1,2,128]{4,1,3,2,0:T(8,128)}, u32[]{:S(2)}) copy-start(f32[2,512,1,2,128]{4,1,3,2,0:T(8,128)} %get-tuple-element.497) | copy-start | bytes 3145732 | tf_op jit(solution)/shard_map/while
Sparse Core Ops, SparseCore 0:
  212.9 54.7 all-gather.2
  270.4 50.5 all-gather.4
  370.5 99.6 reduce-scatter.1
